TPU v7x, 32 devices: a whole 2x2x4 slice. The times are simulated.
32 devices in a mesh: rows: 8 (over z, y), modes: 4 (over x, core).
Axes of the slice: x: 2, y: 2, z: 4, core: 2. Of those that a mesh axis runs over, the one named last changes fastest.
Arguments:
- mode_slab: bfloat16 [4096, 512], P('rows', 'modes'), may hold values from -25 to 25
- mass_diag: float32 [4096], P('rows'), may hold values from 9.5 to 19
- mass_gain: float32 [4096], P('rows'), may hold values from 0.5 to 1.5
- band_coef: float32 [4], replicated, may hold values from 0.2 to 0.5
- band_offsets: int32 [4], replicated, may hold values from 1 to 64, as said below
- boundary_blocks: int32 [16, 4], P('rows'), may hold values from 0 to 31, as said below
- boundary_counts: int32 [16], P('rows'), may hold values from 2 to 4, as said below
- boundary_modes: bfloat16 [16, 512, 512], P('rows'), may hold values from -0.5 to 0.5
Outputs:
- projected: bfloat16 [16, 512, 512], P('rows', 'modes')
Inputs may be any that keep to these rules, and one draw needn't show every extreme that they name: `band_offsets`: the offsets are distinct and one of them equals 64. `boundary_blocks`: entries of one component are distinct. For component c with e = c // 2, every entry b (used or not) satisfies (b - e * 4 + 512 // 256) mod (32) < 8. Among the used entries of the components of each index e of rows, one is the block just below e's rows and one the block just above them, counted cyclically. `boundary_counts`: some component uses all 4 blocks.
All inputs are finite; a program needn't handle non-finite values.
Results may differ from a plain program's by a relative error of at most 0.0035.
The roundings to bfloat16 on the way count: a program that leaves them out, or rounds other values in their place, can miss the bound.
Values may be sent and summed in bfloat16 or wider, within the bound.
No kernel may reach another device: no remote copies, remote signals or barrier semaphores. Data moves between devices by JAX's collectives and lax.ppermute only.
A program may use at most 64 MiB of HBM per device.

v0:
```python
import jax
import jax.numpy as jnp
from jax import lax
from jax.sharding import PartitionSpec as P

CB = 512
BLOCK = 128
BMAX = 4
NOFF = 4
BAND = 64


def padded_2(block, sides, width, periodic):
    for axis, dim in sides:
        count = lax.axis_size(axis)
        forward = [(i, i + 1) for i in range(count - 1)]
        if periodic:
            forward.append((count - 1, 0))
        backward = [(target, source) for source, target in forward]
        low = lax.ppermute(
            lax.slice_in_dim(block, block.shape[dim] - width, None, axis=dim), axis, forward
        )
        high = lax.ppermute(lax.slice_in_dim(block, 0, width, axis=dim), axis, backward)
        block = jnp.concatenate([low, block, high], axis=dim)
    return block


def local(
    mode_slab,
    mass_diag,
    mass_gain,
    band_coef,
    band_offsets,
    boundary_blocks,
    boundary_counts,
    boundary_modes,
):
    rows_dev, mode_cols = mode_slab.shape
    per_dev = rows_dev // BLOCK
    rim_rows = per_dev // 2 * BLOCK
    slab_float = mode_slab.astype(jnp.float32)
    scaled = (mass_gain[:, None] * slab_float).astype(jnp.bfloat16)
    padded = padded_2(scaled, (("rows", 0),), BAND, False)
    neighbour = jnp.zeros((rows_dev, mode_cols), jnp.float32)
    for j in range(NOFF):
        offset = band_offsets[j]
        upward = lax.dynamic_slice_in_dim(padded, BAND + offset, rows_dev, 0)
        downward = lax.dynamic_slice_in_dim(padded, BAND - offset, rows_dev, 0)
        neighbour = neighbour + band_coef[j] * (
            upward.astype(jnp.float32) + downward.astype(jnp.float32)
        )
    mass_image = (mass_diag[:, None] * slab_float + mass_gain[:, None] * neighbour).astype(
        jnp.bfloat16
    )
    every_mode = lax.all_gather(mass_image, "modes", axis=1, tiled=True)
    full_order = every_mode.shape[1]
    total_rows = rows_dev * lax.axis_size("rows")
    partial_value = (
        lax.dot_general(
            every_mode, mode_slab, (((0,), (0,)), ((), ())), preferred_element_type=jnp.float32
        )
        / total_rows
    )
    column_block = lax.psum(partial_value, "rows")
    gram_matrix = lax.all_gather(column_block, "modes", axis=1, tiled=True)
    lower_factor = jnp.linalg.cholesky(gram_matrix)
    first_column = lax.axis_index("modes") * mode_cols
    unit_columns = (
        lax.broadcasted_iota(jnp.int32, (full_order, mode_cols), 0)
        == lax.broadcasted_iota(jnp.int32, (full_order, mode_cols), 1) + first_column
    ).astype(jnp.float32)
    inverse = jax.scipy.linalg.solve_triangular(
        lower_factor, unit_columns, lower=True, trans=1
    ).astype(jnp.bfloat16)
    mass_basis = jnp.dot(every_mode, inverse, preferred_element_type=jnp.float32).astype(
        jnp.bfloat16
    )
    extended = padded_2(mass_basis, (("rows", 0),), rim_rows, True)
    total_blocks = per_dev * lax.axis_size("rows")
    window_start = lax.axis_index("rows") * per_dev - per_dev // 2
    local_blocks = jnp.mod(boundary_blocks - window_start, total_blocks)
    owned = boundary_modes.shape[0]
    shaped = boundary_modes.reshape(owned, BMAX, BLOCK, CB)
    row_index = local_blocks[:, :, None] * BLOCK + jnp.arange(BLOCK, dtype=jnp.int32)[None, None, :]
    picked = jnp.take(extended, row_index, axis=0)
    in_use = jnp.arange(BMAX, dtype=jnp.int32)[None, :] < boundary_counts[:, None]
    picked = jnp.where(in_use[:, :, None, None], picked, jnp.zeros_like(picked))
    result = jnp.einsum("csbk,csbm->ckm", picked, shaped, preferred_element_type=jnp.float32)
    return result.astype(jnp.bfloat16)


def solution(mesh):
    in_specs = (
        P("rows", "modes"),
        P("rows"),
        P("rows"),
        P(),
        P(),
        P("rows", None),
        P("rows"),
        P("rows", None, None),
    )
    out_specs = P("rows", "modes", None)
    return jax.shard_map(local, mesh=mesh, in_specs=in_specs, out_specs=out_specs, check_vma=False)
```

profile of v0, /device:TPU:0, one launch (start us, length us, event | category | flops | bytes accessed | tf_op | source)
XLA Modules:
  0.0 294.4 jit_solution(5894387732189599143)
XLA Ops:
  6.5 1.1 fusion.4
  7.7 4.9 %collective-permute-start = (bf16[64,128]{1,0:T(8,128)(2,1)S(1)}, bf16[64,128]{1,0:T(8,128)(2,1)S(1)}, u32[]{:S(2)}, u32[]{:S(2)}) collective-permute-start(bf16[64,128]{1,0:T(8,128)(2,1)S(1)} %get-tuple-element.25), channel_id=1, source_target_pairs={{0,4},{4,8},{8,12},{12,16},{16,20},{20,24},{24,28},{1,5},{5,9},{9,... | collective-permute-start | bytes 49160 | tf_op jit(solution)/shard_map/ppermute | solution.py:20
  12.6 1.3 collective-permute-start.1
  26.4 2.8 fusion.3
  29.2 7.2 %all_gather.6 = bf16[512,512]{1,0:T(8,128)(2,1)S(1)} all-gather(bf16[512,128]{1,0:T(8,128)(2,1)S(1)} %fusion.3), channel_id=1, replica_groups=mesh['rows'=8,'modes'=4] {'modes'}, dimensions={1}, use_global_device_ids=true | all-gather | bytes 655360 | tf_op jit(solution)/shard_map/all_gather | solution.py:55
  37.3 1.0 convolution_multiply_fusion
  38.3 72.4 %all-reduce.3.cloned.1.call-done = f32[512,128]{0,1:T(8,128)} async-done(((f32[512,128]{0,1:T(8,128)}), f32[512,128]{0,1:T(8,128)}) %all-reduce.3.cloned.1.call-update) | async-done | bytes 262160 | tf_op jit(solution)/shard_map/psum | solution.py:64
  112.8 15.5 %all-gather.2.cloned.1.call-done = f32[512,512]{0,1:T(8,128)} async-done(((f32[512,128]{0,1:T(8,128)}), f32[512,512]{0,1:T(8,128)}) %all-gather.2.cloned.1.call-update) | async-done | bytes 1048592 | tf_op jit(solution)/shard_map/all_gather | solution.py:65
  128.4 1.6 copy.13
  130.3 1.0 copy-done.2
  131.3 11.7 %cholesky.104 = f32[128,128]{1,0:T(8,128)S(1)} custom-call(f32[128,128]{1,0:T(8,128)S(1)} %cholesky.266), custom_call_target="Cholesky" | custom-call | tf_op jit(solution)/shard_map/jit(cholesky)/cholesky | solution.py:66
  143.1 9.8 %custom-call.31 = f32[1,128,128]{1,2,0:T(8,128)S(1)} custom-call(f32[1,128,128]{2,1,0:T(8,128)S(1)} %get-tuple-element.36), custom_call_target="InvertDiagBlocksLowerTriangular" | custom-call | tf_op jit(solution)/shard_map/jit(cholesky)/cholesky | solution.py:66
  154.3 11.7 %cholesky.217 = f32[128,128]{1,0:T(8,128)S(1)} custom-call(f32[128,128]{1,0:T(8,128)S(1)} %cholesky.270), custom_call_target="Cholesky" | custom-call | tf_op jit(solution)/shard_map/jit(cholesky)/cholesky | solution.py:66
  166.1 9.9 %custom-call.32 = f32[1,128,128]{1,2,0:T(8,128)S(1)} custom-call(f32[1,128,128]{2,1,0:T(8,128)S(1)} %get-tuple-element.33), custom_call_target="InvertDiagBlocksLowerTriangular" | custom-call | tf_op jit(solution)/shard_map/jit(cholesky)/cholesky | solution.py:66
  176.0 1.2 convolution_dynamic-update-slice_fusion
  178.2 13.2 %cholesky.238 = f32[128,128]{1,0:T(8,128)} custom-call(f32[128,128]{1,0:T(8,128)} %cholesky.275), custom_call_target="Cholesky" | custom-call | tf_op jit(solution)/shard_map/jit(cholesky)/cholesky | solution.py:66
  191.4 1.5 select_reduce_fusion.1
  193.6 11.3 %custom-call.33 = f32[1,128,128]{1,2,0:T(8,128)} custom-call(f32[1,128,128]{2,1,0:T(8,128)} %get-tuple-element.30), custom_call_target="InvertDiagBlocksLowerTriangular" | custom-call | tf_op jit(solution)/shard_map/jit(cholesky)/cholesky | solution.py:66
  204.8 1.0 convolution_dynamic-update-slice_fusion.1
  206.3 11.7 %cholesky.255 = f32[128,128]{1,0:T(8,128)S(1)} custom-call(f32[128,128]{1,0:T(8,128)S(1)} %convolution_subtract_fusion.5), custom_call_target="Cholesky" | custom-call | tf_op jit(solution)/shard_map/jit(cholesky)/cholesky | solution.py:66
  222.8 9.9 %while.1 = (s32[]{:T(128)}, f32[512,512]{1,0:T(8,128)S(1)}, s32[4,2]{0,1:T(2,128)S(1)}, f32[4,128,128]{2,1,0:T(8,128)}, s32[]{:T(128)}) while((s32[]{:T(128)}, f32[512,512]{1,0:T(8,128)S(1)}, s32[4,2]{0,1:T(2,128)S(1)}, f32[4,128,128]{2,1,0:T(8,128)}, s32[]{:T(128)}) %tuple.39), condition=%wide.while_cond, body=%wide.while_body.sunk | while | flops 2 | bytes 132705 | solution.py:72
  223.4 1.9 bitcast_dynamic-update-slice_fusion.2
  225.8 1.9 bitcast_dynamic-update-slice_fusion.2
  228.3 1.9 bitcast_dynamic-update-slice_fusion.2
  230.8 1.9 bitcast_dynamic-update-slice_fusion.2
  232.6 40.1 %custom-call.34 = f32[4,128,128]{1,2,0:T(8,128)S(1)} custom-call(f32[4,128,128]{2,1,0:T(8,128)} %get-tuple-element.12), custom_call_target="InvertDiagBlocksLowerTriangular" | custom-call | tf_op jit(solution)/shard_map/jit(_solve_triangular)/triangular_solve | solution.py:72
  272.8 0.9 fusion.60
  275.9 1.5 collective-permute-start.2
  277.4 3.3 %collective-permute-start.3 = (bf16[256,128]{1,0:T(8,128)(2,1)S(1)}, bf16[256,128]{1,0:T(8,128)(2,1)S(1)}, u32[]{:S(2)}, u32[]{:S(2)}) collective-permute-start(bf16[256,128]{1,0:T(8,128)(2,1)S(1)} %get-tuple-element.24), channel_id=1, source_target_pairs={{4,0},{8,4},{12,8},{16,12},{20,16},{24,20},{28,24},{0,28},{5,1},{9... | collective-permute-start | bytes 196616 | tf_op jit(solution)/shard_map/ppermute | solution.py:23
  280.8 2.2 collective-permute-done.2
  283.1 3.2 %gather_fusion = bf16[1024,128]{1,0:T(8,128)(2,1)S(1)} fusion(bf16[1024,128]{1,0:T(8,128)(2,1)S(1)} %pad_maximum_fusion, s32[1024]{0:T(1024)S(1)} %broadcast_clamp_fusion), kind=kCustom, calls=%fused_computation | custom fusion | bytes 528384 | tf_op jit(solution)/shard_map/jit(_take)/gather | solution.py:85
  286.5 1.1 fusion
  (84 shorter events, 16.3 us)
Async XLA Ops:
  6.5 280.0 %copy-start = (bf16[2,512,512]{2,1,0:T(8,128)(2,1)S(1)}, bf16[2,512,512]{2,1,0:T(8,128)(2,1)}, u32[]{:S(2)}) copy-start(bf16[2,512,512]{2,1,0:T(8,128)(2,1)} %param.15) | copy-start | bytes 3145732
  6.5 104.1 %all-reduce.3.cloned.1.call-start = ((), (), s32[]{:S(2)}) async-start(), calls=%async_computation | async-start | bytes 524288 | tf_op jit(solution)/shard_map/psum | solution.py:64
  7.7 6.2 %copy-start.9 = (s32[4]{0:T(128)S(1)}, s32[4]{0:T(128)}, u32[]{:S(2)}) copy-start(s32[4]{0:T(128)} %param.12) | copy-start | bytes 52
  7.7 17.8 %collective-permute-start = (bf16[64,128]{1,0:T(8,128)(2,1)S(1)}, bf16[64,128]{1,0:T(8,128)(2,1)S(1)}, u32[]{:S(2)}, u32[]{:S(2)}) collective-permute-start(bf16[64,128]{1,0:T(8,128)(2,1)S(1)} %get-tuple-element.25), channel_id=1, source_target_pairs={{0,4},{4,8},{8,12},{12,16},{16,20},{20,24},{24,28},{1,5},{5,9},{9,... | collective-permute-start | bytes 49160 | tf_op jit(solution)/shard_map/ppermute | solution.py:20
  12.6 12.9 %collective-permute-start.1 = (bf16[64,128]{1,0:T(8,128)(2,1)S(1)}, bf16[64,128]{1,0:T(8,128)(2,1)S(1)}, u32[]{:S(2)}, u32[]{:S(2)}) collective-permute-start(bf16[64,128]{1,0:T(8,128)(2,1)S(1)} %get-tuple-element.26), channel_id=1, source_target_pairs={{4,0},{8,4},{12,8},{16,12},{20,16},{24,20},{28,24},{5,1},{9,5},{13... | collective-permute-start | bytes 49160 | tf_op jit(solution)/shard_map/ppermute | solution.py:23
  13.9 0.7 copy-start.10
  25.5 0.9 copy-start.6
  25.6 0.9 copy-start.11
  25.6 0.8 copy-start.8
  36.4 0.8 copy-start.4
  38.3 90.1 %all-gather.2.cloned.1.call-start = ((), (), s32[]{:S(2)}) async-start(), calls=%async_computation.1 | async-start | bytes 1310720 | tf_op jit(solution)/shard_map/all_gather | solution.py:65
  111.3 0.7 copy-start.12
  128.4 1.7 copy-start.1
  130.2 1.0 copy-start.2
  131.2 21.7 %copy-start.3 = (f32[512,512]{1,0:T(8,128)S(1)}, f32[512,512]{1,0:T(8,128)}, u32[]{:S(2)}) copy-start(f32[512,512]{1,0:T(8,128)} %copy-done.2) | copy-start | bytes 3145732
  153.6 0.7 copy-start.7
  222.1 0.7 copy-start.14
  274.5 1.0 copy-start.5
  275.9 4.8 %copy-start.13 = (s32[2]{0:T(128)S(1)}, s32[2]{0:T(128)}, u32[]{:S(2)}) copy-start(s32[2]{0:T(128)} %param.14) | copy-start | bytes 28
  275.9 7.1 %collective-permute-start.2 = (bf16[256,128]{1,0:T(8,128)(2,1)S(1)}, bf16[256,128]{1,0:T(8,128)(2,1)S(1)}, u32[]{:S(2)}, u32[]{:S(2)}) collective-permute-start(bf16[256,128]{1,0:T(8,128)(2,1)S(1)} %get-tuple-element.23), channel_id=1, source_target_pairs={{0,4},{4,8},{8,12},{12,16},{16,20},{20,24},{24,28},{28,0},{1,5},{5... | collective-permute-start | bytes 196616 | tf_op jit(solution)/shard_map/ppermute | solution.py:20
  277.4 5.7 %collective-permute-start.3 = (bf16[256,128]{1,0:T(8,128)(2,1)S(1)}, bf16[256,128]{1,0:T(8,128)(2,1)S(1)}, u32[]{:S(2)}, u32[]{:S(2)}) collective-permute-start(bf16[256,128]{1,0:T(8,128)(2,1)S(1)} %get-tuple-element.24), channel_id=1, source_target_pairs={{4,0},{8,4},{12,8},{16,12},{20,16},{24,20},{28,24},{0,28},{5,1},{9... | collective-permute-start | bytes 196616 | tf_op jit(solution)/shard_map/ppermute | solution.py:23
Sparse Core Ops, SparseCore 0:
  38.4 72.2 all-reduce.2
  112.3 15.9 all-gather.1
where the time goes:
time: 295 us; the launch traced here: 294 us
  other arithmetic  129 us (44%)
  waiting for transfers between devices  90.3 us (31%)
  between operations  26.6 us (9%)
  local copies, waits for them, and re-layouts  21.7 us (7%)
  starting transfers between devices  11 us (4%)
  matrix products  8.59 us (3%)
  blocking collectives  7.2 us (2%)
    another operation x14, other arithmetic, local(): lower_factor = jnp.linalg.cholesky(gram_matrix)  83.2 us
    psum x1, waiting for transfers between devices, local(): column_block = lax.psum(partial_value, 'rows')  72.4 us
    another operation x3, other arithmetic, local(): jax.scipy.linalg.solve_triangular(lower_factor, unit_columns, lower=True,...  40.8 us
    all_gather x1, waiting for transfers between devices, local(): gram_matrix = lax.all_gather(column_block, 'modes', axis=1, tiled=True)  15.5 us
    another operation x12, local copies, waits for them, and re-layouts  9.85 us
    all_gather x1, blocking collectives, local(): every_mode = lax.all_gather(mass_image, 'modes', axis=1, tiled=True)  7.2 us
    ppermute x2, starting transfers between devices, padded_2(): lax.ppermute(lax.slice_in_dim(block, block.shape[dim] - width, None, axis...  6.39 us
  transfers between devices with their start and end apart: 6, of which 4 were waited for; matrix products, arithmetic and copies ran while one was open for 1% of the time, Pallas kernels for 0%

commit v1 on v0

--- a/solution.py
+++ b/solution.py
@@ -61,7 +61,7 @@
         )
         / total_rows
     )
-    column_block = lax.psum(partial_value, "rows")
+    column_block = jnp.sum(lax.all_gather(partial_value, "rows"), axis=0)
     gram_matrix = lax.all_gather(column_block, "modes", axis=1, tiled=True)
     lower_factor = jnp.linalg.cholesky(gram_matrix)
     first_column = lax.axis_index("modes") * mode_cols

time: 295 us -> 271 us (0.919)
  waiting for transfers between devices: 90.3 us -> 68.6 us
  other arithmetic: 129 us -> 126 us
    psum x1 -> x0, waiting for transfers between devices: 72.4 us -> none  [local(): column_block = lax.psum(partial_value, 'rows')]
    all_gather x0 -> x1, waiting for transfers between devices: none -> 51.1 us  [local(): column_block = jnp.sum(lax.all_gather(partial_value, 'rows'), axis=0)]
    another operation x14, other arithmetic: 83.2 us -> 78.7 us  [local(): lower_factor = jnp.linalg.cholesky(gram_matrix)]
where the time goes in v1:
time: 271 us; the launch traced here: 270 us
  other arithmetic  126 us (46%)
  waiting for transfers between devices  68.6 us (25%)
  between operations  25.9 us (10%)
  local copies, waits for them, and re-layouts  21.1 us (8%)
  starting transfers between devices  11 us (4%)
  matrix products  9.82 us (4%)
  blocking collectives  7.2 us (3%)
    another operation x14, other arithmetic, local(): lower_factor = jnp.linalg.cholesky(gram_matrix)  78.7 us
    all_gather x1, waiting for transfers between devices, local(): column_block = jnp.sum(lax.all_gather(partial_value, 'rows'), axis=0)  51.1 us
    another operation x3, other arithmetic, local(): jax.scipy.linalg.solve_triangular(lower_factor, unit_columns, lower=True,...  40.3 us
    all_gather x1, waiting for transfers between devices, local(): gram_matrix = lax.all_gather(column_block, 'modes', axis=1, tiled=True)  15.1 us
    another operation x12, local copies, waits for them, and re-layouts  10.4 us
    all_gather x1, blocking collectives, local(): every_mode = lax.all_gather(mass_image, 'modes', axis=1, tiled=True)  7.2 us
    ppermute x2, starting transfers between devices, padded_2(): lax.ppermute(lax.slice_in_dim(block, block.shape[dim] - width, None, axis...  6.4 us
    another operation x6, matrix products, local(): lower_factor = jnp.linalg.cholesky(gram_matrix)  5.46 us
  transfers between devices with their start and end apart: 6, of which 4 were waited for; matrix products, arithmetic and copies ran while one was open for 1% of the time, Pallas kernels for 0%

profile of v1, /device:TPU:0, one launch (start us, length us, event | category | flops | bytes accessed | tf_op | source)
XLA Modules:
  0.0 269.8 jit_solution(7855664000502833058)
XLA Ops:
  6.5 1.1 fusion.4
  7.7 4.9 %collective-permute-start = (bf16[64,128]{1,0:T(8,128)(2,1)S(1)}, bf16[64,128]{1,0:T(8,128)(2,1)S(1)}, u32[]{:S(2)}, u32[]{:S(2)}) collective-permute-start(bf16[64,128]{1,0:T(8,128)(2,1)S(1)} %get-tuple-element.25), channel_id=1, source_target_pairs={{0,4},{4,8},{8,12},{12,16},{16,20},{20,24},{24,28},{1,5},{5,9},{9,... | collective-permute-start | bytes 49160 | tf_op jit(solution)/shard_map/ppermute | solution.py:20
  12.6 1.3 collective-permute-start.1
  13.9 1.5 fusion.59
  15.3 1.5 fusion.58
  26.4 3.8 %fusion.3 = bf16[512,128]{1,0:T(8,128)(2,1)S(1)} fusion(bf16[512,128]{1,0:T(8,128)(2,1)} %param.8, bf16[640,128]{1,0:T(8,128)(2,1)S(1)} %pad_maximum_fusion.1, s32[]{:T(128)S(6)} %select_n.68, s32[]{:T(128)S(6)} %select_n.67, f32[]{:T(128)} %bitcast.15, s32[]{:T(128)S(6)} %select_n.66, s32[]{:T(128)S(6)} %select_n.65, f32[]{:T(128)} %bitcast.10, ...), kind=kLoop, calls=%fused_computation.23 | loop fusion | flops 1572864 | bytes 1314864 | tf_op jit(solution)/shard_map/convert_element_type | solution.py:52
  30.2 7.2 %all_gather.12 = bf16[512,512]{1,0:T(8,128)(2,1)S(1)} all-gather(bf16[512,128]{1,0:T(8,128)(2,1)S(1)} %fusion.3), channel_id=1, replica_groups=mesh['rows'=8,'modes'=4] {'modes'}, dimensions={1}, use_global_device_ids=true | all-gather | bytes 655360 | tf_op jit(solution)/shard_map/all_gather | solution.py:55
  39.3 51.1 %all-gather.6.cloned.1.call-done = f32[4096,128]{1,0:T(8,128)} async-done(((f32[512,128]{1,0:T(8,128)}), f32[4096,128]{1,0:T(8,128)}) %all-gather.6.cloned.1.call-update) | async-done | bytes 2097168 | tf_op jit(solution)/shard_map/all_gather | solution.py:64
  90.4 1.7 reduce_sum.9
  93.3 15.1 %all-gather.4.cloned.1.call-done = f32[512,512]{0,1:T(8,128)} async-done(((f32[512,128]{0,1:T(8,128)}), f32[512,512]{0,1:T(8,128)}) %all-gather.4.cloned.1.call-update) | async-done | bytes 1048592 | tf_op jit(solution)/shard_map/all_gather | solution.py:65
  108.4 1.6 copy.14
  111.3 11.7 %cholesky.104 = f32[128,128]{1,0:T(8,128)S(1)} custom-call(f32[128,128]{1,0:T(8,128)S(1)} %cholesky.266), custom_call_target="Cholesky" | custom-call | tf_op jit(solution)/shard_map/jit(cholesky)/cholesky | solution.py:66
  123.1 9.8 %custom-call.31 = f32[1,128,128]{1,2,0:T(8,128)S(1)} custom-call(f32[1,128,128]{2,1,0:T(8,128)S(1)} %get-tuple-element.36), custom_call_target="InvertDiagBlocksLowerTriangular" | custom-call | tf_op jit(solution)/shard_map/jit(cholesky)/cholesky | solution.py:66
  133.0 1.2 constant_dynamic-update-slice_fusion
  134.2 1.3 convolution_subtract_fusion
  135.5 11.7 %cholesky.217 = f32[128,128]{1,0:T(8,128)S(1)} custom-call(f32[128,128]{1,0:T(8,128)S(1)} %cholesky.270), custom_call_target="Cholesky" | custom-call | tf_op jit(solution)/shard_map/jit(cholesky)/cholesky | solution.py:66
  147.2 10.0 %custom-call.32 = f32[1,128,128]{1,2,0:T(8,128)S(1)} custom-call(f32[1,128,128]{2,1,0:T(8,128)S(1)} %get-tuple-element.33), custom_call_target="InvertDiagBlocksLowerTriangular" | custom-call | tf_op jit(solution)/shard_map/jit(cholesky)/cholesky | solution.py:66
  157.5 1.3 convolution_subtract_fusion.1
  158.8 11.7 %cholesky.238 = f32[128,128]{1,0:T(8,128)S(1)} custom-call(f32[128,128]{1,0:T(8,128)S(1)} %cholesky.275), custom_call_target="Cholesky" | custom-call | tf_op jit(solution)/shard_map/jit(cholesky)/cholesky | solution.py:66
  171.2 9.8 %custom-call.33 = f32[1,128,128]{1,2,0:T(8,128)S(1)} custom-call(f32[1,128,128]{2,1,0:T(8,128)S(1)} %get-tuple-element.30), custom_call_target="InvertDiagBlocksLowerTriangular" | custom-call | tf_op jit(solution)/shard_map/jit(cholesky)/cholesky | solution.py:66
  181.2 1.2 convolution_subtract_fusion.5
  182.4 11.9 %cholesky.255 = f32[128,128]{1,0:T(8,128)S(1)} custom-call(f32[128,128]{1,0:T(8,128)S(1)} %convolution_subtract_fusion.5), custom_call_target="Cholesky" | custom-call | tf_op jit(solution)/shard_map/jit(cholesky)/cholesky | solution.py:66
  198.4 10.4 %while.1 = (s32[]{:T(128)}, f32[512,512]{1,0:T(8,128)S(1)}, s32[4,2]{0,1:T(2,128)S(1)}, f32[4,128,128]{2,1,0:T(8,128)}, s32[]{:T(128)}) while((s32[]{:T(128)}, f32[512,512]{1,0:T(8,128)S(1)}, s32[4,2]{0,1:T(2,128)S(1)}, f32[4,128,128]{2,1,0:T(8,128)}, s32[]{:T(128)}) %tuple.39), condition=%wide.while_cond, body=%wide.while_body.sunk | while | flops 2 | bytes 132705 | solution.py:72
  199.0 2.0 bitcast_dynamic-update-slice_fusion.2
  201.6 2.0 bitcast_dynamic-update-slice_fusion.2
  204.2 2.0 bitcast_dynamic-update-slice_fusion.2
  206.8 2.0 bitcast_dynamic-update-slice_fusion.2
  208.8 40.1 %custom-call.34 = f32[4,128,128]{1,2,0:T(8,128)S(1)} custom-call(f32[4,128,128]{2,1,0:T(8,128)} %get-tuple-element.12), custom_call_target="InvertDiagBlocksLowerTriangular" | custom-call | tf_op jit(solution)/shard_map/jit(_solve_triangular)/triangular_solve | solution.py:72
  251.3 1.5 collective-permute-start.2
  252.8 3.2 %collective-permute-start.3 = (bf16[256,128]{1,0:T(8,128)(2,1)S(1)}, bf16[256,128]{1,0:T(8,128)(2,1)S(1)}, u32[]{:S(2)}, u32[]{:S(2)}) collective-permute-start(bf16[256,128]{1,0:T(8,128)(2,1)S(1)} %get-tuple-element.24), channel_id=1, source_target_pairs={{4,0},{8,4},{12,8},{16,12},{20,16},{24,20},{28,24},{0,28},{5,1},{9... | collective-permute-start | bytes 196616 | tf_op jit(solution)/shard_map/ppermute | solution.py:23
  256.1 2.2 collective-permute-done.2
  258.5 3.2 %gather_fusion = bf16[1024,128]{1,0:T(8,128)(2,1)S(1)} fusion(bf16[1024,128]{1,0:T(8,128)(2,1)S(1)} %pad_maximum_fusion, s32[1024]{0:T(1024)S(1)} %broadcast_clamp_fusion), kind=kCustom, calls=%fused_computation | custom fusion | bytes 528384 | tf_op jit(solution)/shard_map/jit(_take)/gather | solution.py:85
  (72 shorter events, 13.3 us)
Async XLA Ops:
  6.5 255.4 %copy-start = (bf16[2,512,512]{2,1,0:T(8,128)(2,1)S(1)}, bf16[2,512,512]{2,1,0:T(8,128)(2,1)}, u32[]{:S(2)}) copy-start(bf16[2,512,512]{2,1,0:T(8,128)(2,1)} %param.15) | copy-start | bytes 3145732
  6.5 31.7 %copy-start.5 = (bf16[512,128]{1,0:T(8,128)(2,1)S(1)}, bf16[512,128]{1,0:T(8,128)(2,1)}, u32[]{:S(2)}) copy-start(bf16[512,128]{1,0:T(8,128)(2,1)} %param.8) | copy-start | bytes 393220
  6.5 83.9 %all-gather.6.cloned.1.call-start = ((), (), s32[]{:S(2)}) async-start(), calls=%async_computation.1 | async-start | bytes 2359296 | tf_op jit(solution)/shard_map/all_gather | solution.py:64
  7.7 18.7 %collective-permute-start = (bf16[64,128]{1,0:T(8,128)(2,1)S(1)}, bf16[64,128]{1,0:T(8,128)(2,1)S(1)}, u32[]{:S(2)}, u32[]{:S(2)}) collective-permute-start(bf16[64,128]{1,0:T(8,128)(2,1)S(1)} %get-tuple-element.25), channel_id=1, source_target_pairs={{0,4},{4,8},{8,12},{12,16},{16,20},{20,24},{24,28},{1,5},{5,9},{9,... | collective-permute-start | bytes 49160 | tf_op jit(solution)/shard_map/ppermute | solution.py:20
  12.6 13.8 %collective-permute-start.1 = (bf16[64,128]{1,0:T(8,128)(2,1)S(1)}, bf16[64,128]{1,0:T(8,128)(2,1)S(1)}, u32[]{:S(2)}, u32[]{:S(2)}) collective-permute-start(bf16[64,128]{1,0:T(8,128)(2,1)S(1)} %get-tuple-element.26), channel_id=1, source_target_pairs={{4,0},{8,4},{12,8},{16,12},{20,16},{24,20},{28,24},{5,1},{9,5},{13... | collective-permute-start | bytes 49160 | tf_op jit(solution)/shard_map/ppermute | solution.py:23
  37.4 0.8 copy-start.3
  38.2 54.9 %copy-start.6 = (s32[2,4]{1,0:T(2,128)S(1)}, s32[2,4]{1,0:T(2,128)}, u32[]{:S(2)}) copy-start(s32[2,4]{1,0:T(2,128)} %param.13) | copy-start | bytes 100
  39.3 69.1 %all-gather.4.cloned.1.call-start = ((), (), s32[]{:S(2)}) async-start(), calls=%async_computation | async-start | bytes 1310720 | tf_op jit(solution)/shard_map/all_gather | solution.py:65
  108.4 1.7 copy-start.1
  110.3 1.0 copy-start.2
  198.4 52.6 %copy-start.4 = (bf16[512,512]{1,0:T(8,128)(2,1)S(1)}, bf16[512,512]{1,0:T(8,128)(2,1)}, u32[]{:S(2)}) copy-start(bf16[512,512]{1,0:T(8,128)(2,1)} %copy-done.3) | copy-start | bytes 1572868
  198.4 57.7 %copy-start.7 = (s32[2]{0:T(128)S(1)}, s32[2]{0:T(128)}, u32[]{:S(2)}) copy-start(s32[2]{0:T(128)} %param.14) | copy-start | bytes 28
  251.3 7.1 %collective-permute-start.2 = (bf16[256,128]{1,0:T(8,128)(2,1)S(1)}, bf16[256,128]{1,0:T(8,128)(2,1)S(1)}, u32[]{:S(2)}, u32[]{:S(2)}) collective-permute-start(bf16[256,128]{1,0:T(8,128)(2,1)S(1)} %get-tuple-element.23), channel_id=1, source_target_pairs={{0,4},{4,8},{8,12},{12,16},{16,20},{20,24},{24,28},{28,0},{1,5},{5... | collective-permute-start | bytes 196616 | tf_op jit(solution)/shard_map/ppermute | solution.py:20
  252.8 5.7 %collective-permute-start.3 = (bf16[256,128]{1,0:T(8,128)(2,1)S(1)}, bf16[256,128]{1,0:T(8,128)(2,1)S(1)}, u32[]{:S(2)}, u32[]{:S(2)}) collective-permute-start(bf16[256,128]{1,0:T(8,128)(2,1)S(1)} %get-tuple-element.24), channel_id=1, source_target_pairs={{4,0},{8,4},{12,8},{16,12},{20,16},{24,20},{28,24},{0,28},{5,1},{9... | collective-permute-start | bytes 196616 | tf_op jit(solution)/shard_map/ppermute | solution.py:23
Sparse Core Ops, SparseCore 0:
  39.4 51.0 all-gather.5
  93.2 15.1 all-gather.3
